TPU v7x, 32 devices: a whole 2x2x4 slice. The times are simulated.
32 devices in a mesh: img: 8 (over y, x, core), head: 4 (over z).
Axes of the slice: x: 2, y: 2, z: 4, core: 2. Of those that a mesh axis runs over, the one named last changes fastest.
Arguments:
- tokens: bfloat16 [40, 256, 768], P('img'), may hold values from -6 to 6
- mask_embed: float32 [768], replicated, may hold values from -6 to 6
- norm_gains: float32 [2, 768], replicated, may hold values from 0.1 to 1.9
- norm_shifts: float32 [2, 768], replicated, may hold values from -4 to 4
- qkv_weight: bfloat16 [3, 768, 768], P(None, None, 'head'), may hold values from -0.3125 to 0.3125
- qv_bias: float32 [2, 768], P(None, 'head'), may hold values from -4 to 4
- out_weight: bfloat16 [768, 768], P('head'), may hold values from -0.4375 to 0.4375
- output_biases: float32 [2, 768], replicated, may hold values from -4 to 4
- up_weight: bfloat16 [768, 3072], P(None, 'head'), may hold values from -0.21875 to 0.21875
- up_bias: float32 [3072], P('head'), may hold values from -4 to 4
- down_weight: bfloat16 [3072, 768], P('head'), may hold values from -0.109375 to 0.109375
- counts: int32 [40], P('img'), may hold values from 1 to 256, as said below
- token_ranks: int32 [40, 256], P('img'), may hold values from 0 to 255, each once within a row
- cotangent: bfloat16 [40, 256, 768], P('img'), may hold values from -6 to 6
Outputs:
- out: bfloat16 [40, 256, 768], P('img')
- tokens_grad: float32 [40, 256, 768], P('img')
- mask_embed_grad: float32 [768], replicated
- norm_gains_grad: float32 [2, 768], replicated
- norm_shifts_grad: float32 [2, 768], replicated
- qkv_weight_grad: float32 [3, 768, 768], P(None, None, 'head')
- qv_bias_grad: float32 [2, 768], P(None, 'head')
- out_weight_grad: float32 [768, 768], P('head')
- output_biases_grad: float32 [2, 768], replicated
- up_weight_grad: float32 [768, 3072], P(None, 'head')
- up_bias_grad: float32 [3072], P('head')
- down_weight_grad: float32 [3072, 768], P('head')
Inputs may be any that keep to these rules, and one draw needn't show every extreme that they name: `counts`: each image's count follows the cosine masking plan over 256 tokens. `token_ranks`: each image's row is a permutation of 0 to 255.
All inputs are finite; a program needn't handle non-finite values.
Results may differ from a plain program's by a relative error of at most 0.012.
The roundings to bfloat16 on the way count: a program that leaves them out, or rounds other values in their place, can miss the bound.
Values sent between devices are 32-bit elements; how exact they have to be, the bound alone decides.
No kernel may reach another device: no remote copies, remote signals or barrier semaphores. Data moves between devices by JAX's collectives and lax.ppermute only.
A program may use at most 128 MiB of HBM per device.

v0:
```python
from functools import partial

import jax
import jax.numpy as jnp
from jax import lax
from jax.sharding import PartitionSpec as P

HEAD_DIM = 48


norm_eps = 1e-06


def contract_rows(left, right):
    return lax.dot_general(
        left, right, (((0,), (0,)), ((), ())), preferred_element_type=jnp.float32
    )


def times_transposed(left, right):
    return lax.dot_general(
        left, right, (((1,), (1,)), ((), ())), preferred_element_type=jnp.float32
    )


def normalize(values, scaling, offset):
    center = values - jnp.mean(values, axis=-1, keepdims=True)
    inverse = lax.rsqrt(jnp.mean(center * center, axis=-1, keepdims=True) + norm_eps)
    normal = center * inverse
    return (normal * scaling + offset, normal, inverse)


def normalize_back(upstream, normal, inverse, scaling):
    scaled = upstream * scaling
    inner = (
        scaled
        - jnp.mean(scaled, axis=-1, keepdims=True)
        - normal * jnp.mean(scaled * normal, axis=-1, keepdims=True)
    )
    return (inverse * inner, jnp.sum(upstream * normal, axis=0), jnp.sum(upstream, axis=0))


def forward(start, params, images, seq_len):
    (
        norm_gains,
        norm_shifts,
        qkv_weight,
        qv_bias,
        out_weight,
        output_biases,
        up_weight,
        up_bias,
        down_weight,
    ) = params
    local_width = qkv_weight.shape[2]
    head_shape = (images, seq_len, local_width // HEAD_DIM, HEAD_DIM)
    score_scale = HEAD_DIM ** (-0.5)
    attn_normed, attn_normal, attn_inverse = normalize(start, norm_gains[0], norm_shifts[0])
    attn_normed = attn_normed.astype(jnp.bfloat16)
    bias_rows = jnp.stack([qv_bias[0], jnp.zeros_like(qv_bias[0]), qv_bias[1]])
    projected = jnp.einsum(
        "td,ndc->ntc", attn_normed, qkv_weight, preferred_element_type=jnp.float32
    )
    projected = (projected + bias_rows[:, None, :]).astype(jnp.bfloat16)
    scores = (
        jnp.einsum(
            "bqhd,bkhd->bhqk",
            projected[0].reshape(head_shape),
            projected[1].reshape(head_shape),
            preferred_element_type=jnp.float32,
        )
        * score_scale
    )
    row_max = jnp.max(scores, axis=-1, keepdims=True)
    exponent = jnp.exp(scores - row_max)
    row_total = jnp.sum(exponent, axis=-1, keepdims=True)
    attn_probs = (exponent / row_total).astype(jnp.bfloat16)
    log_total = row_max + jnp.log(row_total)
    mixed = jnp.einsum(
        "bhqk,bkhd->bqhd",
        attn_probs,
        projected[2].reshape(head_shape),
        preferred_element_type=jnp.float32,
    )
    mixed = mixed.reshape(start.shape[0], local_width).astype(jnp.bfloat16)
    attended = lax.psum(jnp.dot(mixed, out_weight, preferred_element_type=jnp.float32), "head")
    after_attn = start + attended + output_biases[0]
    mlp_normed, mlp_normal, mlp_inverse = normalize(after_attn, norm_gains[1], norm_shifts[1])
    mlp_normed = mlp_normed.astype(jnp.bfloat16)
    pre_act = jnp.dot(mlp_normed, up_weight, preferred_element_type=jnp.float32) + up_bias
    activated = jax.nn.gelu(pre_act, approximate=True).astype(jnp.bfloat16)
    branch = lax.psum(jnp.dot(activated, down_weight, preferred_element_type=jnp.float32), "head")
    after_mlp = after_attn + branch + output_biases[1]
    saved = (
        attn_normal,
        attn_inverse,
        attn_normed,
        projected,
        log_total,
        mixed,
        mlp_normal,
        mlp_inverse,
        mlp_normed,
        pre_act,
        activated,
    )
    return (after_mlp, saved)


def per_device(
    tokens,
    mask_embed,
    norm_gains,
    norm_shifts,
    qkv_weight,
    qv_bias,
    out_weight,
    output_biases,
    up_weight,
    up_bias,
    down_weight,
    counts,
    token_ranks,
    cotangent,
):
    images, seq_len, model_width = tokens.shape
    row_count = images * seq_len
    local_width = qkv_weight.shape[2]
    head_shape = (images, seq_len, local_width // HEAD_DIM, HEAD_DIM)
    score_scale = HEAD_DIM ** (-0.5)
    local_count = jnp.sum(counts.astype(jnp.float32))
    masked_sum = lax.psum(local_count, "img")
    is_masked = (token_ranks < counts[:, None]).reshape(row_count, 1)
    mask_col = is_masked.astype(jnp.float32)
    start = jnp.where(
        is_masked, mask_embed[None, :], tokens.reshape(row_count, model_width).astype(jnp.float32)
    )
    params = (
        norm_gains,
        norm_shifts,
        qkv_weight,
        qv_bias,
        out_weight,
        output_biases,
        up_weight,
        up_bias,
        down_weight,
    )
    result, saved = forward(start, params, images, seq_len)
    again = lax.optimization_barrier((start, result))[0]
    unused, saved = forward(again, params, images, seq_len)
    (
        attn_normal,
        attn_inverse,
        attn_normed,
        projected,
        log_total,
        mixed,
        mlp_normal,
        mlp_inverse,
        mlp_normed,
        pre_act,
        activated,
    ) = saved
    signal = cotangent.reshape(row_count, model_width).astype(jnp.float32) * mask_col
    signal_low = signal.astype(jnp.bfloat16)
    down_bias_raw = jnp.sum(signal, axis=0)
    down_weight_raw = contract_rows(activated, signal_low)
    grad_act = times_transposed(signal_low, down_weight)
    unused_value, gelu_pull = jax.vjp(partial(jax.nn.gelu, approximate=True), pre_act)
    grad_pre = gelu_pull(grad_act)[0].astype(jnp.bfloat16)
    up_bias_raw = jnp.sum(grad_pre.astype(jnp.float32), axis=0)
    up_weight_raw = contract_rows(mlp_normed, grad_pre)
    grad_mlp_normed = lax.psum(times_transposed(grad_pre, up_weight), "head")
    grad_after, mlp_gain_raw, mlp_shift_raw = normalize_back(
        grad_mlp_normed, mlp_normal, mlp_inverse, norm_gains[1]
    )
    upper = signal + grad_after
    upper_low = upper.astype(jnp.bfloat16)
    out_bias_raw = jnp.sum(upper, axis=0)
    out_weight_raw = contract_rows(mixed, upper_low)
    grad_mixed = times_transposed(upper_low, out_weight).astype(jnp.bfloat16).reshape(head_shape)
    queries = projected[0].reshape(head_shape)
    keys_local = projected[1].reshape(head_shape)
    values_local = projected[2].reshape(head_shape)
    scores = (
        jnp.einsum("bqhd,bkhd->bhqk", queries, keys_local, preferred_element_type=jnp.float32)
        * score_scale
    )
    probs = jnp.exp(scores - log_total)
    probs_low = probs.astype(jnp.bfloat16)
    grad_probs = jnp.einsum(
        "bqhd,bkhd->bhqk", grad_mixed, values_local, preferred_element_type=jnp.float32
    )
    grad_values = jnp.einsum(
        "bhqk,bqhd->bkhd", probs_low, grad_mixed, preferred_element_type=jnp.float32
    )
    inner_sum = jnp.sum(probs * grad_probs, axis=-1, keepdims=True)
    grad_scores = (probs * (grad_probs - inner_sum) * score_scale).astype(jnp.bfloat16)
    grad_queries = jnp.einsum(
        "bhqk,bkhd->bqhd", grad_scores, keys_local, preferred_element_type=jnp.float32
    )
    grad_keys = jnp.einsum(
        "bhqk,bqhd->bkhd", grad_scores, queries, preferred_element_type=jnp.float32
    )
    grad_project = (
        jnp.stack([grad_queries, grad_keys, grad_values])
        .reshape(3, row_count, local_width)
        .astype(jnp.bfloat16)
    )
    qkv_weight_raw = jnp.einsum(
        "td,ntc->ndc", attn_normed, grad_project, preferred_element_type=jnp.float32
    )
    column_sums = jnp.sum(grad_project.astype(jnp.float32), axis=1)
    qv_bias_raw = jnp.stack([column_sums[0], column_sums[2]])
    grad_attn_normed = lax.psum(
        jnp.einsum("ntc,ndc->td", grad_project, qkv_weight, preferred_element_type=jnp.float32),
        "head",
    )
    grad_start, attn_gain_raw, attn_shift_raw = normalize_back(
        grad_attn_normed, attn_normal, attn_inverse, norm_gains[0]
    )
    lower = upper + grad_start
    mask_embed_raw = jnp.sum(lower * mask_col, axis=0)
    tokens_raw = lower * (1.0 - mask_col)
    gains_raw = jnp.stack([attn_gain_raw, mlp_gain_raw])
    shifts_raw = jnp.stack([attn_shift_raw, mlp_shift_raw])
    biases_raw = jnp.stack([out_bias_raw, down_bias_raw])
    summed = lax.psum(
        (
            mask_embed_raw,
            gains_raw,
            shifts_raw,
            qkv_weight_raw,
            qv_bias_raw,
            out_weight_raw,
            biases_raw,
            up_weight_raw,
            up_bias_raw,
            down_weight_raw,
        ),
        "img",
    )
    loss_scale = lax.axis_size("img") * row_count / masked_sum
    out = result.astype(jnp.bfloat16).reshape(images, seq_len, model_width)
    tokens_grad = (tokens_raw * loss_scale).reshape(images, seq_len, model_width)
    return (
        out,
        tokens_grad,
        summed[0] * loss_scale,
        summed[1] * loss_scale,
        summed[2] * loss_scale,
        summed[3] * loss_scale,
        summed[4] * loss_scale,
        summed[5] * loss_scale,
        summed[6] * loss_scale,
        summed[7] * loss_scale,
        summed[8] * loss_scale,
        summed[9] * loss_scale,
    )


def solution(mesh):
    return jax.shard_map(
        per_device,
        mesh=mesh,
        in_specs=(
            P("img", None, None),
            P(),
            P(),
            P(),
            P(None, None, "head"),
            P(None, "head"),
            P("head", None),
            P(),
            P(None, "head"),
            P("head"),
            P("head", None),
            P("img"),
            P("img", None),
            P("img", None, None),
        ),
        out_specs=(
            P("img", None, None),
            P("img", None, None),
            P(),
            P(),
            P(),
            P(None, None, "head"),
            P(None, "head"),
            P("head", None),
            P(),
            P(None, "head"),
            P("head"),
            P("head", None),
        ),
        check_vma=False,
    )
```

profile of v0, /device:TPU:0, one launch (start us, length us, event | category | flops | bytes accessed | tf_op | source)
XLA Modules:
  0.0 1022.0 jit_solution(18225187835026592122)
XLA Ops:
  23.9 5.7 fusion.141
  36.3 149.1 %all-reduce.9.cloned.1.call-done = f32[1280,768]{1,0:T(8,128)} async-done(((f32[1280,768]{1,0:T(8,128)}), f32[1280,768]{1,0:T(8,128)}) %all-reduce.9.cloned.1.call-update) | async-done | bytes 3932176 | tf_op jit(solution)/shard_map/psum | solution.py:86
  191.1 7.2 fusion.89
  198.3 145.6 %all-reduce.11.cloned.1.call-done = f32[1280,768]{1,0:T(8,128)} async-done(((f32[1280,768]{1,0:T(8,128)}), f32[1280,768]{1,0:T(8,128)}) %all-reduce.11.cloned.1.call-update) | async-done | bytes 3932176 | tf_op jit(solution)/shard_map/psum | solution.py:92
  343.9 5.1 add_add_fusion.1
  373.4 3.7 fusion.153
  377.1 140.0 %all-reduce.13.cloned.1.call-done = f32[1280,768]{1,0:T(8,128)} async-done(((f32[1280,768]{1,0:T(8,128)}), f32[1280,768]{1,0:T(8,128)}) %all-reduce.13.cloned.1.call-update) | async-done | bytes 3932176 | tf_op jit(solution)/shard_map/psum | solution.py:86
  517.1 3.8 fusion.135
  524.5 6.0 convert_reduce_fusion
  531.7 3.7 fusion.154
  535.8 145.2 %all-reduce.15.cloned.1.call-done = f32[1280,768]{1,0:T(8,128)} async-done(((f32[1280,768]{1,0:T(8,128)}), f32[1280,768]{1,0:T(8,128)}) %all-reduce.15.cloned.1.call-update) | async-done | bytes 3932176 | tf_op jit(solution)/shard_map/psum | solution.py:174
  681.0 4.7 multiply_reduce_fusion.4
  693.4 4.4 fusion.94
  697.7 4.3 fusion.76
  702.1 10.6 %fusion.82 = bf16[5,256,4,48]{1,3,2,0:T(8,128)(2,1)} fusion(f32[5,4,256,256]{2,3,1,0:T(8,128)} %fusion.94, f32[5,4,256,256]{2,3,1,0:T(8,128)} %copy-done.10, f32[5,4,256]{2,1,0:T(4,128)S(1)} %log_add_fusion, bf16[5,256,4,48]{1,0,3,2:T(8,128)(2,1)} %copy-done.23), kind=kOutput, calls=%fused_computation.104 | convolution fusion | flops 137876736 | bytes 11489280 | tf_op jit(solution)/shard_map/bhqk,bkhd->bqhd/dot_general | solution.py:200
  712.7 9.4 fusion.79
  734.4 4.8 convolution_bitcast_fusion
  739.3 6.4 fusion.131
  745.8 3.5 fusion.58
  757.0 127.9 %all-reduce.17.cloned.1.call-done = f32[1280,768]{1,0:T(8,128)} async-done(((f32[1280,768]{1,0:T(8,128)}), f32[1280,768]{1,0:T(8,128)}) %all-reduce.17.cloned.1.call-update) | async-done | bytes 3932176 | tf_op jit(solution)/shard_map/psum | solution.py:216
  884.9 5.2 multiply_reduce_fusion.5
  890.5 4.7 multiply_reduce_fusion.6
  895.2 26.4 %all-reduce = (f32[]{:T(128)}, f32[768]{0:T(1024)S(1)}, f32[2,768]{1,0:T(2,128)S(1)}, f32[2,768]{1,0:T(2,128)S(1)}, f32[2,192]{1,0:T(2,128)S(1)}, /*index=5*/f32[2,768]{1,0:T(2,128)S(1)}, f32[768]{0:T(1024)S(1)}) all-reduce(f32[]{:T(128)} %convert_reduce_fusion.2, ...), channel_id=1, replica_groups=mesh['img'=8,'head'=4] {'img'}, use_global_device_ids=true, to_apply=%region_23.24 | all-reduce | flops 6529 | bytes 52232 | tf_op jit(solution)/shard_map/psum | solution.py:132
  922.3 79.6 %all-reduce.19.cloned.1.call-done = (f32[3,768,192]{1,2,0:T(8,128)}, f32[192,768]{1,0:T(8,128)}, f32[768,768]{1,0:T(8,128)}, f32[768,768]{1,0:T(8,128)}) async-done(((f32[3,768,192]{1,2,0:T(8,128)}, f32[192,768]{1,0:T(8,128)}, f32[768,768]{1,0:T(8,128)}, f32[768,768]{1,0:T(8,128)}), (f32[3,768,192]{1,2,0:T(8,128)}, f32[192,768]{1,0:T(8,128)}, f32[768,768]{1,0:T(8,128)}, ...) | async-done | bytes 7077904 | tf_op jit(solution)/shard_map/psum | solution.py:229
  (197 shorter events, 99.3 us)
Async XLA Ops:
  7.2 183.9 %copy-start = (bf16[768,768]{1,0:T(8,128)(2,1)S(1)}, bf16[768,768]{1,0:T(8,128)(2,1)}, u32[]{:S(2)}) copy-start(bf16[768,768]{1,0:T(8,128)(2,1)} %param.22) | copy-start | bytes 3538948
  7.2 5.5 copy-start.31
  7.2 5.5 copy-start.12
  7.2 5.5 copy-start.35
  7.2 178.2 %all-reduce.9.cloned.1.call-start = ((), (), s32[]{:S(2)}) async-start(), calls=%async_computation | async-start | bytes 7864320 | tf_op jit(solution)/shard_map/psum | solution.py:86
  29.6 3.8 copy-start.18
  36.1 307.8 %all-reduce.11.cloned.1.call-start = ((), (), s32[]{:S(2)}) async-start(), calls=%async_computation.1 | async-start | bytes 7864320 | tf_op jit(solution)/shard_map/psum | solution.py:92
  198.3 318.8 %all-reduce.13.cloned.1.call-start = ((), (), s32[]{:S(2)}) async-start(), calls=%async_computation.2 | async-start | bytes 7864320 | tf_op jit(solution)/shard_map/psum | solution.py:86
  358.7 7.6 copy-start.22
  360.6 5.7 copy-start.23
  371.4 309.6 %all-reduce.15.cloned.1.call-start = ((), (), s32[]{:S(2)}) async-start(), calls=%async_computation.3 | async-start | bytes 7864320 | tf_op jit(solution)/shard_map/psum | solution.py:174
  520.9 9.5 copy-start.8
  520.9 3.5 copy-start.42
  535.4 349.5 %all-reduce.17.cloned.1.call-start = ((), (), s32[]{:S(2)}) async-start(), calls=%async_computation.4 | async-start | bytes 7864320 | tf_op jit(solution)/shard_map/psum | solution.py:216
  681.0 4.7 copy-start.9
  681.0 5.6 copy-start.15
  702.1 10.6 %copy-start.24 = (bf16[5,256,4,48]{1,0,3,2:T(8,128)(2,1)S(1)}, bf16[5,256,4,48]{1,0,3,2:T(8,128)(2,1)}, u32[]{:S(2)}) copy-start(bf16[5,256,4,48]{1,0,3,2:T(8,128)(2,1)} %reshape_squeeze.25) | copy-start | bytes 1474564
  739.3 262.6 %all-reduce.19.cloned.1.call-start = ((), (), s32[]{:S(2)}) async-start(), calls=%async_computation.5 | async-start | bytes 14155776 | tf_op jit(solution)/shard_map/psum | solution.py:229
  739.3 6.5 copy-start.28
  739.3 6.5 copy-start.43
  884.9 5.3 copy-start.4
  884.9 5.6 copy-start.7
  1001.9 4.9 copy-start.30
  1005.3 7.3 copy-start.14
  (27 other events, 57.9 us)
Sparse Core Ops, SparseCore 0:
  36.2 149.2 all-reduce.8
  198.4 145.4 all-reduce.10
  371.6 145.4 all-reduce.12
  535.5 145.4 all-reduce.14
  739.4 145.4 all-reduce.16
  889.6 112.2 all-reduce.18
where the time goes:
time: 1030 us; the launch traced here: 1020 us
  waiting for transfers between devices  787 us (76%)
  matrix products  90.1 us (9%)
  other arithmetic  58.6 us (6%)
  local copies, waits for them, and re-layouts  42.6 us (4%)
  blocking collectives  26.4 us (3%)
  between operations  15.8 us (2%)
    psum x2, waiting for transfers between devices, forward(): lax.psum(jnp.dot(mixed, out_weight, preferred_element_type=jnp.float32),...  289 us
    psum x1, waiting for transfers between devices, forward(): lax.psum(jnp.dot(activated, down_weight, preferred_element_type=jnp.float...  146 us
    psum x1, waiting for transfers between devices, per_device(): grad_mlp_normed = lax.psum(times_transposed(grad_pre, up_weight), 'head')  145 us
    psum x1, waiting for transfers between devices, per_device(): lax.psum(jnp.einsum('ntc,ndc->td', grad_project, qkv_weight, preferred_el...  128 us
    psum x1, waiting for transfers between devices, per_device(): lax.psum((mask_embed_raw, gains_raw, shifts_raw, qkv_weight_raw, qv_bias_...  79.6 us
    psum x1, blocking collectives, per_device(): masked_sum = lax.psum(local_count, 'img')  26.4 us
  transfers between devices with their start and end apart: 6, of which 6 were waited for; matrix products, arithmetic and copies ran while one was open for 3% of the time, Pallas kernels for 0%

commit v1 on v0

v1 whole, which is shorter than its diff:
```python
import jax
import jax.numpy as jnp
from jax import lax
from jax.sharding import PartitionSpec as P

HEAD_DIM = 48
norm_eps = 1e-06
f32 = jnp.float32
bf16 = jnp.bfloat16


def contract_rows(left, right):
    return lax.dot_general(left, right, (((0,), (0,)), ((), ())), preferred_element_type=f32)


def times_transposed(left, right):
    return lax.dot_general(left, right, (((1,), (1,)), ((), ())), preferred_element_type=f32)


def times(left, right):
    return jnp.dot(left, right, preferred_element_type=f32)


def normal_of(values):
    center = values - jnp.mean(values, axis=-1, keepdims=True)
    inverse = lax.rsqrt(jnp.mean(center * center, axis=-1, keepdims=True) + norm_eps)
    return center * inverse, inverse


def normalize_back(upstream, normal, inverse, scaling):
    scaled = upstream * scaling
    inner = (
        scaled
        - jnp.mean(scaled, axis=-1, keepdims=True)
        - normal * jnp.mean(scaled * normal, axis=-1, keepdims=True)
    )
    return inverse * inner


def head_sum(part):
    if lax.axis_size("head") != 4:
        return lax.psum(part, "head")
    place = lax.axis_index("head")
    inner = (place == 1) | (place == 2)
    half = part + lax.ppermute(part, "head", [(0, 1), (3, 2)])
    total = half + lax.ppermute(half, "head", [(1, 2), (2, 1)])
    return jnp.where(inner, total, lax.ppermute(total, "head", [(1, 0), (2, 3)]))


def gelu_and_slope(v):
    k = 0.7978845608028654
    th = jnp.tanh(k * (v + 0.044715 * (v * v * v)))
    act = 0.5 * v * (1.0 + th)
    slope = 0.5 * (1.0 + th) + 0.5 * v * (1.0 - th * th) * (k * (1.0 + 3 * 0.044715 * (v * v)))
    return act, slope


def per_device(
    tokens, mask_embed, norm_gains, norm_shifts, qkv_weight, qv_bias, out_weight, output_biases,
    up_weight, up_bias, down_weight, counts, token_ranks, cotangent,
):
    images, seq_len, model_width = tokens.shape
    local_width = qkv_weight.shape[2]
    heads = local_width // HEAD_DIM
    scale = HEAD_DIM ** (-0.5)
    split = lambda m: m.reshape(seq_len, heads, HEAD_DIM).transpose(1, 0, 2)
    merge = lambda m: m.transpose(1, 0, 2).reshape(seq_len, local_width)
    bdot = lambda a, b, ca, cb: lax.dot_general(
        a, b, (((ca,), (cb,)), ((0,), (0,))), preferred_element_type=f32
    )

    masked_sum = lax.psum(jnp.sum(counts.astype(f32)), "img")
    loss_scale = lax.axis_size("img") * images * seq_len / masked_sum
    is_masked = token_ranks < counts[:, None]

    st = []
    for b in range(images):
        mask = is_masked[b][:, None]
        start = jnp.where(mask, mask_embed[None, :], tokens[b].astype(f32))
        normal, inverse = normal_of(start)
        normed = (normal * norm_gains[0] + norm_shifts[0]).astype(bf16)
        q = split((times(normed, qkv_weight[0]) + qv_bias[0]).astype(bf16))
        k = split(times(normed, qkv_weight[1]).astype(bf16))
        v = split((times(normed, qkv_weight[2]) + qv_bias[1]).astype(bf16))
        scores = bdot(q, k, 2, 2) * scale
        ex = jnp.exp(scores - jnp.max(scores, axis=-1, keepdims=True))
        probs = ex / jnp.sum(ex, axis=-1, keepdims=True)
        mixed = merge(bdot(probs.astype(bf16), v, 2, 1)).astype(bf16)
        attended = head_sum(times(mixed, out_weight))
        st.append(dict(mask=mask.astype(f32), start=start, normal=normal, inverse=inverse,
                       normed=normed, q=q, k=k, v=v, probs=probs, mixed=mixed, attended=attended))
    for b, s in enumerate(st):
        after = s["start"] + s["attended"] + output_biases[0]
        normal, inverse = normal_of(after)
        normed = (normal * norm_gains[1] + norm_shifts[1]).astype(bf16)
        act, slope = gelu_and_slope(times(normed, up_weight) + up_bias)
        act = act.astype(bf16)
        signal = cotangent[b].astype(f32) * s["mask"]
        signal_low = signal.astype(bf16)
        grad_pre = (times_transposed(signal_low, down_weight) * slope).astype(bf16)
        grad_normed = head_sum(times_transposed(grad_pre, up_weight))
        s.update(after=after, normal2=normal, inverse2=inverse, normed2=normed, act=act,
                 signal=signal, signal_low=signal_low, grad_pre=grad_pre, grad_normed2=grad_normed)
    for b, s in enumerate(st):
        upper = s["signal"] + normalize_back(s["grad_normed2"], s["normal2"], s["inverse2"], norm_gains[1])
        upper_low = upper.astype(bf16)
        gm = split(times_transposed(upper_low, out_weight).astype(bf16))
        probs = s["probs"]
        gp = bdot(gm, s["v"], 2, 2)
        gv = merge(bdot(probs.astype(bf16), gm, 1, 1)).astype(bf16)
        gs = (probs * (gp - jnp.sum(probs * gp, axis=-1, keepdims=True)) * scale).astype(bf16)
        gq = merge(bdot(gs, s["k"], 2, 1)).astype(bf16)
        gk = merge(bdot(gs, s["q"], 1, 1)).astype(bf16)
        back = (times_transposed(gq, qkv_weight[0]) + times_transposed(gk, qkv_weight[1])
                + times_transposed(gv, qkv_weight[2]))
        s.update(upper=upper, upper_low=upper_low, gq=gq, gk=gk, gv=gv, grad_normed1=head_sum(back))
    for b, s in enumerate(st):
        s["branch"] = head_sum(times(s["act"], down_weight))
        s["out"] = (s["after"] + s["branch"] + output_biases[1]).astype(bf16)

    cat = lambda name: jnp.concatenate([s[name] for s in st], axis=0)
    down_raw = contract_rows(cat("act"), cat("signal_low"))
    up_raw = contract_rows(cat("normed2"), cat("grad_pre"))
    down_raw, up_raw = lax.psum((down_raw, up_raw), "img")
    out_raw = contract_rows(cat("mixed"), cat("upper_low"))
    normed1 = cat("normed")
    qkv_raw = jnp.stack([contract_rows(normed1, cat(n)) for n in ("gq", "gk", "gv")])
    out_raw, qkv_raw = lax.psum((out_raw, qkv_raw), "img")

    total = lambda f: sum(f(s) for s in st)
    sums = lambda m: jnp.sum(m.astype(f32), axis=0)
    for s in st:
        grad = normalize_back(s["grad_normed1"], s["normal"], s["inverse"], norm_gains[0])
        s["lower"] = s["upper"] + grad
    small = [
        total(lambda s: sums(s["lower"] * s["mask"])),
        total(lambda s: sums(s["grad_normed1"] * s["normal"])),
        total(lambda s: sums(s["grad_normed2"] * s["normal2"])),
        total(lambda s: sums(s["grad_normed1"])),
        total(lambda s: sums(s["grad_normed2"])),
        total(lambda s: sums(s["upper"])),
        total(lambda s: sums(s["signal"])),
    ]
    small = jnp.stack(small)
    bias = jnp.concatenate([total(lambda s: sums(s["gq"])), total(lambda s: sums(s["gv"])),
                            total(lambda s: sums(s["grad_pre"]))])
    small, bias = lax.psum((small, bias), "img")
    small = small * loss_scale
    bias = bias * loss_scale
    out = jnp.stack([s["out"] for s in st])
    tokens_grad = jnp.stack([s["lower"] * ((1.0 - s["mask"]) * loss_scale) for s in st])
    return (
        out,
        tokens_grad,
        small[0],
        small[1:3],
        small[3:5],
        qkv_raw * loss_scale,
        bias[: 2 * local_width].reshape(2, local_width),
        out_raw * loss_scale,
        small[5:7],
        up_raw * loss_scale,
        bias[2 * local_width :],
        down_raw * loss_scale,
    )


def solution(mesh):
    return jax.shard_map(
        per_device,
        mesh=mesh,
        in_specs=(
            P("img", None, None), P(), P(), P(), P(None, None, "head"), P(None, "head"),
            P("head", None), P(), P(None, "head"), P("head"), P("head", None), P("img"),
            P("img", None), P("img", None, None),
        ),
        out_specs=(
            P("img", None, None), P("img", None, None), P(), P(), P(), P(None, None, "head"),
            P(None, "head"), P("head", None), P(), P(None, "head"), P("head"), P("head", None),
        ),
        check_vma=False,
    )
```

time: 1030 us -> 873 us (0.85)
  waiting for transfers between devices: 787 us -> 454 us
  starting transfers between devices: 1.04 us -> 89.8 us
  matrix products: 90.1 us -> 144 us
  other arithmetic: 58.6 us -> 110 us
  local copies, waits for them, and re-layouts: 42.6 us -> 19.5 us
    psum x6 -> x1, waiting for transfers between devices: 787 us -> 39.8 us  [per_device(): out_raw, qkv_raw = lax.psum((out_raw, qkv_raw), 'img')]
    ppermute x0 -> x60, waiting for transfers between devices: none -> 415 us  [the longest x20 251 us: head_sum(): lax.ppermute(total, 'head', [(1, 0), (2, 3)])]
    ppermute x0 -> x60, starting transfers between devices: none -> 89.8 us  [the longest x20 42.8 us: head_sum(): half = part + lax.ppermute(part, 'head', [(0, 1), (3, 2)])]
    dot_general x13 -> x55, matrix products: 61.1 us -> 91 us  [the longest x25 65.7 us: per_device(): lax.dot_general(a, b, (((ca,), (cb,)), ((0,), (0,))), preferred_element_t...]
    unnamed x0 -> x22, other arithmetic: none -> 26.7 us
    add x2 -> x50, other arithmetic: 5.15 us -> 28.5 us  [the longest x20 15.9 us: head_sum(): total = half + lax.ppermute(half, 'head', [(1, 2), (2, 1)])]
    another operation x17 -> x1, local copies, waits for them, and re-layouts: 17.1 us -> 0.05 us  [per_device(): small = jnp.stack(small)]
    dot_general x3 -> x30, matrix products: 8.95 us -> 24.5 us  [times_transposed(): lax.dot_general(left, right, (((1,), (1,)), ((), ())), preferred_element_...]
  transfers between devices with their start and end apart: 6 -> 61, of which waited for: 6 -> 31; matrix products, arithmetic and copies ran while one was open for 3% -> 20% of each run, Pallas kernels for 0% -> 0%
where the time goes in v1:
time: 873 us; the launch traced here: 862 us
  waiting for transfers between devices  454 us (52%)
  matrix products  144 us (16%)
  other arithmetic  110 us (13%)
  starting transfers between devices  89.8 us (10%)
  blocking collectives  24.4 us (3%)
  local copies, waits for them, and re-layouts  19.5 us (2%)
  between operations  19.5 us (2%)
    ppermute x20, waiting for transfers between devices, head_sum(): lax.ppermute(total, 'head', [(1, 0), (2, 3)])  251 us
    ppermute x20, waiting for transfers between devices, head_sum(): half = part + lax.ppermute(part, 'head', [(0, 1), (3, 2)])  163 us
    dot_general x25, matrix products, per_device(): lax.dot_general(a, b, (((ca,), (cb,)), ((0,), (0,))), preferred_element_t...  65.7 us
    ppermute x20, starting transfers between devices, head_sum(): half = part + lax.ppermute(part, 'head', [(0, 1), (3, 2)])  42.8 us
    psum x1, waiting for transfers between devices, per_device(): out_raw, qkv_raw = lax.psum((out_raw, qkv_raw), 'img')  39.8 us
    ppermute x20, starting transfers between devices, head_sum(): lax.ppermute(total, 'head', [(1, 0), (2, 3)])  26.9 us
    unnamed x22, other arithmetic  26.7 us
    dot_general x30, matrix products, times(): return jnp.dot(left, right, preferred_element_type=f32)  25.3 us
  transfers between devices with their start and end apart: 61, of which 31 were waited for; matrix products, arithmetic and copies ran while one was open for 20% of the time, Pallas kernels for 0%

profile of v1, /device:TPU:0, one launch (start us, length us, event | category | flops | bytes accessed | tf_op | source)
XLA Modules:
  0.0 862.1 jit_solution(5414913964256480171)
XLA Ops:
  25.0 16.7 %collective-permute-done.12 = f32[256,768]{1,0:T(8,128)S(1)} collective-permute-done((f32[256,768]{1,0:T(8,128)S(1)}, f32[256,768]{1,0:T(8,128)S(1)}, u32[]{:S(2)}, u32[]{:S(2)}) %collective-permute-start.12) | collective-permute-done | bytes 786464 | tf_op jit(solution)/shard_map/ppermute | solution.py:45
  45.6 37.5 %collective-permute-done.14 = f32[256,768]{1,0:T(8,128)} collective-permute-done((f32[256,768]{1,0:T(8,128)}, f32[256,768]{1,0:T(8,128)}, u32[]{:S(2)}, u32[]{:S(2)}) %collective-permute-start.14) | collective-permute-done | bytes 786464 | tf_op jit(solution)/shard_map/ppermute | solution.py:47
  90.8 14.6 %collective-permute-done.42 = f32[256,768]{1,0:T(8,128)S(1)} collective-permute-done((f32[256,768]{1,0:T(8,128)S(1)}, f32[256,768]{1,0:T(8,128)S(1)}, u32[]{:S(2)}, u32[]{:S(2)}) %collective-permute-start.42) | collective-permute-done | bytes 786464 | tf_op jit(solution)/shard_map/ppermute | solution.py:45
  107.7 33.6 %collective-permute-done.44 = f32[256,768]{1,0:T(8,128)S(1)} collective-permute-done((f32[256,768]{1,0:T(8,128)S(1)}, f32[256,768]{1,0:T(8,128)S(1)}, u32[]{:S(2)}, u32[]{:S(2)}) %collective-permute-start.44) | collective-permute-done | bytes 786464 | tf_op jit(solution)/shard_map/ppermute | solution.py:47
  161.5 12.4 %collective-permute-done.45 = f32[256,768]{1,0:T(8,128)S(1)} collective-permute-done((f32[256,768]{1,0:T(8,128)S(1)}, f32[256,768]{1,0:T(8,128)S(1)}, u32[]{:S(2)}, u32[]{:S(2)}) %collective-permute-start.45) | collective-permute-done | bytes 786464 | tf_op jit(solution)/shard_map/ppermute | solution.py:45
  176.4 29.0 %collective-permute-done.47 = f32[256,768]{1,0:T(8,128)S(1)} collective-permute-done((f32[256,768]{1,0:T(8,128)S(1)}, f32[256,768]{1,0:T(8,128)S(1)}, u32[]{:S(2)}, u32[]{:S(2)}) %collective-permute-start.47) | collective-permute-done | bytes 786464 | tf_op jit(solution)/shard_map/ppermute | solution.py:47
  231.0 9.5 %collective-permute-done.18 = f32[256,768]{1,0:T(8,128)} collective-permute-done((f32[256,768]{1,0:T(8,128)}, f32[256,768]{1,0:T(8,128)}, u32[]{:S(2)}, u32[]{:S(2)}) %collective-permute-start.18) | collective-permute-done | bytes 786464 | tf_op jit(solution)/shard_map/ppermute | solution.py:45
  253.4 31.2 %collective-permute-done.20 = f32[256,768]{1,0:T(8,128)S(1)} collective-permute-done((f32[256,768]{1,0:T(8,128)S(1)}, f32[256,768]{1,0:T(8,128)S(1)}, u32[]{:S(2)}, u32[]{:S(2)}) %collective-permute-start.20) | collective-permute-done | bytes 786464 | tf_op jit(solution)/shard_map/ppermute | solution.py:47
  284.6 8.4 collective-permute-done.2
  304.1 11.2 %collective-permute-done.48 = f32[256,768]{1,0:T(8,128)S(1)} collective-permute-done((f32[256,768]{1,0:T(8,128)S(1)}, f32[256,768]{1,0:T(8,128)S(1)}, u32[]{:S(2)}, u32[]{:S(2)}) %collective-permute-start.48) | collective-permute-done | bytes 786464 | tf_op jit(solution)/shard_map/ppermute | solution.py:45
  327.8 25.9 %collective-permute-done.50 = f32[256,768]{1,0:T(8,128)S(1)} collective-permute-done((f32[256,768]{1,0:T(8,128)S(1)}, f32[256,768]{1,0:T(8,128)S(1)}, u32[]{:S(2)}, u32[]{:S(2)}) %collective-permute-start.50) | collective-permute-done | bytes 786464 | tf_op jit(solution)/shard_map/ppermute | solution.py:47
  400.9 13.6 %collective-permute-done.33 = f32[256,768]{1,0:T(8,128)S(1)} collective-permute-done((f32[256,768]{1,0:T(8,128)S(1)}, f32[256,768]{1,0:T(8,128)S(1)}, u32[]{:S(2)}, u32[]{:S(2)}) %collective-permute-start.33) | collective-permute-done | bytes 786464 | tf_op jit(solution)/shard_map/ppermute | solution.py:45
  415.5 11.7 %collective-permute-done.51 = f32[256,768]{1,0:T(8,128)S(1)} collective-permute-done((f32[256,768]{1,0:T(8,128)S(1)}, f32[256,768]{1,0:T(8,128)S(1)}, u32[]{:S(2)}, u32[]{:S(2)}) %collective-permute-start.51) | collective-permute-done | bytes 786464 | tf_op jit(solution)/shard_map/ppermute | solution.py:45
  428.0 10.9 %collective-permute-done.15 = f32[256,768]{1,0:T(8,128)S(1)} collective-permute-done((f32[256,768]{1,0:T(8,128)S(1)}, f32[256,768]{1,0:T(8,128)S(1)}, u32[]{:S(2)}, u32[]{:S(2)}) %collective-permute-start.15) | collective-permute-done | bytes 786464 | tf_op jit(solution)/shard_map/ppermute | solution.py:45
  536.5 13.2 %collective-permute-done.26 = f32[256,768]{1,0:T(8,128)S(1)} collective-permute-done((f32[256,768]{1,0:T(8,128)S(1)}, f32[256,768]{1,0:T(8,128)S(1)}, u32[]{:S(2)}, u32[]{:S(2)}) %collective-permute-start.26) | collective-permute-done | bytes 786464 | tf_op jit(solution)/shard_map/ppermute | solution.py:47
  549.7 8.4 collective-permute-done.8
  573.9 10.3 %collective-permute-done.54 = f32[256,768]{1,0:T(8,128)S(1)} collective-permute-done((f32[256,768]{1,0:T(8,128)S(1)}, f32[256,768]{1,0:T(8,128)S(1)}, u32[]{:S(2)}, u32[]{:S(2)}) %collective-permute-start.54) | collective-permute-done | bytes 786464 | tf_op jit(solution)/shard_map/ppermute | solution.py:45
  585.1 14.8 %collective-permute-done.36 = f32[256,768]{1,0:T(8,128)S(1)} collective-permute-done((f32[256,768]{1,0:T(8,128)S(1)}, f32[256,768]{1,0:T(8,128)S(1)}, u32[]{:S(2)}, u32[]{:S(2)}) %collective-permute-start.36) | collective-permute-done | bytes 786464 | tf_op jit(solution)/shard_map/ppermute | solution.py:45
  625.6 16.3 %collective-permute-done.56 = f32[256,768]{1,0:T(8,128)S(1)} collective-permute-done((f32[256,768]{1,0:T(8,128)S(1)}, f32[256,768]{1,0:T(8,128)S(1)}, u32[]{:S(2)}, u32[]{:S(2)}) %collective-permute-start.56) | collective-permute-done | bytes 786464 | tf_op jit(solution)/shard_map/ppermute | solution.py:47
  641.9 14.8 %collective-permute-done.38 = f32[256,768]{1,0:T(8,128)S(1)} collective-permute-done((f32[256,768]{1,0:T(8,128)S(1)}, f32[256,768]{1,0:T(8,128)S(1)}, u32[]{:S(2)}, u32[]{:S(2)}) %collective-permute-start.38) | collective-permute-done | bytes 786464 | tf_op jit(solution)/shard_map/ppermute | solution.py:47
  748.5 8.9 %collective-permute-done.41 = f32[256,768]{1,0:T(8,128)S(1)} collective-permute-done((f32[256,768]{1,0:T(8,128)S(1)}, f32[256,768]{1,0:T(8,128)S(1)}, u32[]{:S(2)}, u32[]{:S(2)}) %collective-permute-start.41) | collective-permute-done | bytes 786464 | tf_op jit(solution)/shard_map/ppermute | solution.py:47
  757.3 8.4 collective-permute-done.59
  773.8 24.4 %all-reduce = (f32[]{:T(128)}, f32[7,768]{1,0:T(8,128)S(1)}, f32[1152]{0:T(1024)S(1)}) all-reduce(f32[]{:T(128)} %convert_reduce_fusion.15, f32[7,768]{1,0:T(8,128)S(1)} %stack.70, f32[1152]{0:T(1024)S(1)} %concatenate.37), channel_id=1, replica_groups=mesh['img'=8,'head'=4] {'img'}, use_global_device_ids=true, to_apply=%region_36.37 | all-reduce | flops 6529 | bytes 52232 | tf_op jit(solution)/shard_map/psum | solution.py:72
  807.7 39.8 %all-reduce.4.cloned.1.call-done = (f32[3,768,192]{1,2,0:T(8,128)}, f32[192,768]{1,0:T(8,128)}, f32[768,768]{1,0:T(8,128)}, f32[768,768]{1,0:T(8,128)}) async-done(((f32[3,768,192]{1,2,0:T(8,128)}, f32[192,768]{1,0:T(8,128)}, f32[768,768]{1,0:T(8,128)}, f32[768,768]{1,0:T(8,128)}), (f32[3,768,192]{1,2,0:T(8,128)}, f32[192,768]{1,0:T(8,128)}, f32[768,768]{1,0:T(8,128)}, ...) | async-done | bytes 7077904 | tf_op jit(solution)/shard_map/psum | solution.py:128
  (934 shorter events, 416.8 us)
Async XLA Ops:
  7.2 840.3 %all-reduce.4.cloned.1.call-start = ((), (), s32[]{:S(2)}) async-start(), calls=%async_computation | async-start | bytes 14155776 | tf_op jit(solution)/shard_map/psum | solution.py:128
  43.6 39.6 %collective-permute-start.14 = (f32[256,768]{1,0:T(8,128)}, f32[256,768]{1,0:T(8,128)}, u32[]{:S(2)}, u32[]{:S(2)}) collective-permute-start(f32[256,768]{1,0:T(8,128)} %add.1054), channel_id=1, source_target_pairs={{1,0},{2,3},{5,4},{6,7},{9,8},{10,11},{13,12},{14,15},{17,16},{18,... | collective-permute-start | bytes 2359304 | tf_op jit(solution)/shard_map/ppermute | solution.py:47
  106.4 34.9 %collective-permute-start.44 = (f32[256,768]{1,0:T(8,128)S(1)}, f32[256,768]{1,0:T(8,128)S(1)}, u32[]{:S(2)}, u32[]{:S(2)}) collective-permute-start(f32[256,768]{1,0:T(8,128)S(1)} %add.1123), channel_id=1, source_target_pairs={{1,0},{2,3},{5,4},{6,7},{9,8},{10,11},{13,12},{14,15},{17,16},{18,... | collective-permute-start | bytes 2359304 | tf_op jit(solution)/shard_map/ppermute | solution.py:47
  174.8 30.5 %collective-permute-start.47 = (f32[256,768]{1,0:T(8,128)S(1)}, f32[256,768]{1,0:T(8,128)S(1)}, u32[]{:S(2)}, u32[]{:S(2)}) collective-permute-start(f32[256,768]{1,0:T(8,128)S(1)} %add.1128), channel_id=1, source_target_pairs={{1,0},{2,3},{5,4},{6,7},{9,8},{10,11},{13,12},{14,15},{17,16},{18,... | collective-permute-start | bytes 2359304 | tf_op jit(solution)/shard_map/ppermute | solution.py:47
  250.6 34.0 %collective-permute-start.20 = (f32[256,768]{1,0:T(8,128)S(1)}, f32[256,768]{1,0:T(8,128)S(1)}, u32[]{:S(2)}, u32[]{:S(2)}) collective-permute-start(f32[256,768]{1,0:T(8,128)S(1)} %add.1071), channel_id=1, source_target_pairs={{1,0},{2,3},{5,4},{6,7},{9,8},{10,11},{13,12},{14,15},{17,16},{18,... | collective-permute-start | bytes 2359304 | tf_op jit(solution)/shard_map/ppermute | solution.py:47
  252.0 41.0 %collective-permute-start.2 = (f32[256,768]{1,0:T(8,128)S(1)}, f32[256,768]{1,0:T(8,128)S(1)}, u32[]{:S(2)}, u32[]{:S(2)}) collective-permute-start(f32[256,768]{1,0:T(8,128)S(1)} %add.1013), channel_id=1, source_target_pairs={{1,0},{2,3},{5,4},{6,7},{9,8},{10,11},{13,12},{14,15},{17,16},{18,... | collective-permute-start | bytes 2359304 | tf_op jit(solution)/shard_map/ppermute | solution.py:47
  324.7 29.0 %collective-permute-start.50 = (f32[256,768]{1,0:T(8,128)S(1)}, f32[256,768]{1,0:T(8,128)S(1)}, u32[]{:S(2)}, u32[]{:S(2)}) collective-permute-start(f32[256,768]{1,0:T(8,128)S(1)} %add.1133), channel_id=1, source_target_pairs={{1,0},{2,3},{5,4},{6,7},{9,8},{10,11},{13,12},{14,15},{17,16},{18,... | collective-permute-start | bytes 2359304 | tf_op jit(solution)/shard_map/ppermute | solution.py:47
  326.1 36.1 %collective-permute-start.32 = (f32[256,768]{1,0:T(8,128)S(1)}, f32[256,768]{1,0:T(8,128)S(1)}, u32[]{:S(2)}, u32[]{:S(2)}) collective-permute-start(f32[256,768]{1,0:T(8,128)S(1)} %add.1103), channel_id=1, source_target_pairs={{1,0},{2,3},{5,4},{6,7},{9,8},{10,11},{13,12},{14,15},{17,16},{18,... | collective-permute-start | bytes 2359304 | tf_op jit(solution)/shard_map/ppermute | solution.py:47
  397.6 29.6 %collective-permute-start.51 = (f32[256,768]{1,0:T(8,128)S(1)}, f32[256,768]{1,0:T(8,128)S(1)}, u32[]{:S(2)}, u32[]{:S(2)}) collective-permute-start(f32[256,768]{1,0:T(8,128)S(1)} %convolution_add_fusion.2), channel_id=1, source_target_pairs={{0,1},{3,2},{4,5},{7,6},{8,9},{11,10},{12,13},{15,14},{16,17},{19,... | collective-permute-start | bytes 2359304 | tf_op jit(solution)/shard_map/ppermute | solution.py:45
  399.6 39.4 %collective-permute-start.15 = (f32[256,768]{1,0:T(8,128)S(1)}, f32[256,768]{1,0:T(8,128)S(1)}, u32[]{:S(2)}, u32[]{:S(2)}) collective-permute-start(f32[256,768]{1,0:T(8,128)S(1)} %fusion.397), channel_id=1, source_target_pairs={{0,1},{3,2},{4,5},{7,6},{8,9},{11,10},{12,13},{15,14},{16,17},{19,... | collective-permute-start | bytes 2359304 | tf_op jit(solution)/shard_map/ppermute | solution.py:45
  414.6 36.0 %collective-permute-start.34 = (f32[256,768]{1,0:T(8,128)S(1)}, f32[256,768]{1,0:T(8,128)S(1)}, u32[]{:S(2)}, u32[]{:S(2)}) collective-permute-start(f32[256,768]{1,0:T(8,128)S(1)} %add.1107), channel_id=1, source_target_pairs={{1,2},{2,1},{5,6},{6,5},{9,10},{10,9},{13,14},{14,13},{17,18},{18,... | collective-permute-start | bytes 2359304 | tf_op jit(solution)/shard_map/ppermute | solution.py:46
  452.2 27.9 %collective-permute-start.53 = (f32[256,768]{1,0:T(8,128)S(1)}, f32[256,768]{1,0:T(8,128)S(1)}, u32[]{:S(2)}, u32[]{:S(2)}) collective-permute-start(f32[256,768]{1,0:T(8,128)S(1)} %add.1138), channel_id=1, source_target_pairs={{1,0},{2,3},{5,4},{6,7},{9,8},{10,11},{13,12},{14,15},{17,16},{18,... | collective-permute-start | bytes 2359304 | tf_op jit(solution)/shard_map/ppermute | solution.py:47
  456.3 287.6 %collective-permute-start.17 = (f32[256,768]{1,0:T(8,128)}, f32[256,768]{1,0:T(8,128)}, u32[]{:S(2)}, u32[]{:S(2)}) collective-permute-start(f32[256,768]{1,0:T(8,128)} %add.1063), channel_id=1, source_target_pairs={{1,0},{2,3},{5,4},{6,7},{9,8},{10,11},{13,12},{14,15},{17,16},{18,... | collective-permute-start | bytes 2359304 | tf_op jit(solution)/shard_map/ppermute | solution.py:47
  461.9 45.8 %collective-permute-start.4 = (f32[256,768]{1,0:T(8,128)}, f32[256,768]{1,0:T(8,128)}, u32[]{:S(2)}, u32[]{:S(2)}) collective-permute-start(f32[256,768]{1,0:T(8,128)} %add.1026), channel_id=1, source_target_pairs={{1,2},{2,1},{5,6},{6,5},{9,10},{10,9},{13,14},{14,13},{17,18},{18,... | collective-permute-start | bytes 2359304 | tf_op jit(solution)/shard_map/ppermute | solution.py:46
  470.4 43.4 %collective-permute-start.22 = (f32[256,768]{1,0:T(8,128)}, f32[256,768]{1,0:T(8,128)}, u32[]{:S(2)}, u32[]{:S(2)}) collective-permute-start(f32[256,768]{1,0:T(8,128)} %add.1079), channel_id=1, source_target_pairs={{1,2},{2,1},{5,6},{6,5},{9,10},{10,9},{13,14},{14,13},{17,18},{18,... | collective-permute-start | bytes 2359304 | tf_op jit(solution)/shard_map/ppermute | solution.py:46
  567.7 32.2 %collective-permute-start.36 = (f32[256,768]{1,0:T(8,128)S(1)}, f32[256,768]{1,0:T(8,128)S(1)}, u32[]{:S(2)}, u32[]{:S(2)}) collective-permute-start(f32[256,768]{1,0:T(8,128)S(1)} %fusion.446), channel_id=1, source_target_pairs={{0,1},{3,2},{4,5},{7,6},{8,9},{11,10},{12,13},{15,14},{16,17},{19,... | collective-permute-start | bytes 2359304 | tf_op jit(solution)/shard_map/ppermute | solution.py:45
  570.4 37.9 %collective-permute-start.9 = (f32[256,768]{1,0:T(8,128)S(1)}, f32[256,768]{1,0:T(8,128)S(1)}, u32[]{:S(2)}, u32[]{:S(2)}) collective-permute-start(f32[256,768]{1,0:T(8,128)S(1)} %fusion.396), channel_id=1, source_target_pairs={{0,1},{3,2},{4,5},{7,6},{8,9},{11,10},{12,13},{15,14},{16,17},{19,... | collective-permute-start | bytes 2359304 | tf_op jit(solution)/shard_map/ppermute | solution.py:45
  572.4 44.3 %collective-permute-start.27 = (f32[256,768]{1,0:T(8,128)S(1)}, f32[256,768]{1,0:T(8,128)S(1)}, u32[]{:S(2)}, u32[]{:S(2)}) collective-permute-start(f32[256,768]{1,0:T(8,128)S(1)} %fusion.399), channel_id=1, source_target_pairs={{0,1},{3,2},{4,5},{7,6},{8,9},{11,10},{12,13},{15,14},{16,17},{19,... | collective-permute-start | bytes 2359304 | tf_op jit(solution)/shard_map/ppermute | solution.py:45
  584.4 33.3 %collective-permute-start.55 = (f32[256,768]{1,0:T(8,128)S(1)}, f32[256,768]{1,0:T(8,128)S(1)}, u32[]{:S(2)}, u32[]{:S(2)}) collective-permute-start(f32[256,768]{1,0:T(8,128)S(1)} %add.1142), channel_id=1, source_target_pairs={{1,2},{2,1},{5,6},{6,5},{9,10},{10,9},{13,14},{14,13},{17,18},{18,... | collective-permute-start | bytes 2359304 | tf_op jit(solution)/shard_map/ppermute | solution.py:46
  619.4 37.2 %collective-permute-start.38 = (f32[256,768]{1,0:T(8,128)S(1)}, f32[256,768]{1,0:T(8,128)S(1)}, u32[]{:S(2)}, u32[]{:S(2)}) collective-permute-start(f32[256,768]{1,0:T(8,128)S(1)} %add.1113), channel_id=1, source_target_pairs={{1,0},{2,3},{5,4},{6,7},{9,8},{10,11},{13,12},{14,15},{17,16},{18,... | collective-permute-start | bytes 2359304 | tf_op jit(solution)/shard_map/ppermute | solution.py:47
  621.0 125.0 %collective-permute-start.23 = (f32[256,768]{1,0:T(8,128)}, f32[256,768]{1,0:T(8,128)}, u32[]{:S(2)}, u32[]{:S(2)}) collective-permute-start(f32[256,768]{1,0:T(8,128)} %add.1080), channel_id=1, source_target_pairs={{1,0},{2,3},{5,4},{6,7},{9,8},{10,11},{13,12},{14,15},{17,16},{18,... | collective-permute-start | bytes 2359304 | tf_op jit(solution)/shard_map/ppermute | solution.py:47
  623.3 117.1 %collective-permute-start.11 = (f32[256,768]{1,0:T(8,128)}, f32[256,768]{1,0:T(8,128)}, u32[]{:S(2)}, u32[]{:S(2)}) collective-permute-start(f32[256,768]{1,0:T(8,128)} %add.1046), channel_id=1, source_target_pairs={{1,0},{2,3},{5,4},{6,7},{9,8},{10,11},{13,12},{14,15},{17,16},{18,... | collective-permute-start | bytes 2359304 | tf_op jit(solution)/shard_map/ppermute | solution.py:47
  734.4 37.1 %collective-permute-start.29 = (f32[256,768]{1,0:T(8,128)}, f32[256,768]{1,0:T(8,128)}, u32[]{:S(2)}, u32[]{:S(2)}) collective-permute-start(f32[256,768]{1,0:T(8,128)} %add.1097), channel_id=1, source_target_pairs={{1,0},{2,3},{5,4},{6,7},{9,8},{10,11},{13,12},{14,15},{17,16},{18,... | collective-permute-start | bytes 2359304 | tf_op jit(solution)/shard_map/ppermute | solution.py:47
  740.4 25.4 %collective-permute-start.59 = (f32[256,768]{1,0:T(8,128)S(1)}, f32[256,768]{1,0:T(8,128)S(1)}, u32[]{:S(2)}, u32[]{:S(2)}) collective-permute-start(f32[256,768]{1,0:T(8,128)S(1)} %add.1148), channel_id=1, source_target_pairs={{1,0},{2,3},{5,4},{6,7},{9,8},{10,11},{13,12},{14,15},{17,16},{18,... | collective-permute-start | bytes 2359304 | tf_op jit(solution)/shard_map/ppermute | solution.py:47
  (304 other events, 4685.9 us)
Sparse Core Ops, SparseCore 0:
  734.4 112.9 all-reduce.3
